TPU v7x, 32 devices: a whole 2x2x4 slice. The times are simulated.
32 devices in a mesh: gx: 4 (over z), yz: 8 (over y, x, core).
Axes of the slice: x: 2, y: 2, z: 4, core: 2. Of those that a mesh axis runs over, the one named last changes fastest.
Arguments:
- positions: bfloat16 [3, 8192], P(None, ('gx', 'yz')), may hold values from 0 to 1
- species: int32 [8192], P(('gx', 'yz')), may hold values from 0 to 5
- features: bfloat16 [8192, 512], P(('gx', 'yz')), may hold values from -6 to 6
- move_dest: int32 [64], P(('gx', 'yz')), may hold values from 0 to 7, as said below
- move_slot: int32 [64], P(('gx', 'yz')), may hold values from 0 to 1, as said below
- halo_list: int32 [1024], P(('gx', 'yz')), may hold values from 0 to 255
- neighbours: int32 [8192, 64], P(('gx', 'yz')), may hold values from 0 to 383, as said below
- neighbour_count: int32 [8192], P(('gx', 'yz')), may hold values from 16 to 64
- wave_index: int32 [3, 4096], replicated, may hold values from -16 to 16, as said below
- radial_in: bfloat16 [8, 64], replicated, may hold values from -2 to 2
- radial_mid: bfloat16 [2, 64, 64], replicated, may hold values from -0.75 to 0.75
- radial_out: bfloat16 [64, 512], replicated, may hold values from -0.75 to 0.75
- up_weight: bfloat16 [2, 128, 128], replicated, may hold values from -0.5 to 0.5
- prod_weight: float32 [6, 640], replicated, may hold values from -4 to 4
- out_weight: bfloat16 [2, 128, 128], replicated, may hold values from -0.5 to 0.5
- skip_weight: bfloat16 [2, 128, 128], replicated, may hold values from -0.5 to 0.5
- charge_weight: bfloat16 [128, 8], replicated, may hold values from -0.5 to 0.5
- field_weight: float32 [8, 128], replicated, may hold values from -2 to 2
- read_weight: bfloat16 [128, 16], replicated, may hold values from -0.5 to 0.5
- read_vector: float32 [16], replicated, may hold values from -1.5 to 1.5
- force_weight: float32 [128], replicated, may hold values from -0.5 to 0.5
Outputs:
- forces: float32 [3, 8192], P(None, ('gx', 'yz'))
- energies: float32 [8192], P(('gx', 'yz'))
Inputs may be any that keep to these rules, and one draw needn't show every extreme that they name: `move_dest`: the destination lies in the same gx row. Exactly 2 blocks of each device go to other devices, at most one to any one device, and each device receives exactly 2 blocks; the others stay. `move_slot`: the 2 blocks that a device holds after the move take its 2 slots once each. `neighbours`: row of the device's table: its working atoms, then the ghosts from gx - 1, gx + 1, yz - 1, yz + 1. Never the atom itself; slots from neighbour_count on are padding. `wave_index`: row 0 runs from 1 to 8, row 1 from -16 to 16, row 2 from -2 to 2.
All inputs are finite; a program needn't handle non-finite values.
Results may differ from a plain program's by a relative error of at most 0.0028.
Values may be sent and summed in bfloat16 or wider, within the bound.
A program may use at most 64 MiB of HBM per device.

v0:
```python
import math
import jax
import jax.numpy as jnp
from jax import lax
from jax.sharding import PartitionSpec as P

highest = lax.Precision.HIGHEST
two_pi = 2.0 * math.pi
cutoff_radius = 3.5
basis_sharpness = 4.0
ewald_width = 0.1
ewald_scale = 0.01
atom_step = 64
wave_step = 512


def with_halo(value, sides, width):
    for axis, dim in sides:
        count, length = (lax.axis_size(axis), value.shape[dim])
        up = [(i, (i + 1) % count) for i in range(count)]
        down = [(j, i) for i, j in up]
        last = lax.slice_in_dim(value, length - width, length, axis=dim)
        leading = lax.slice_in_dim(value, 0, width, axis=dim)
        before = lax.ppermute(last, axis, up)
        after = lax.ppermute(leading, axis, down)
        value = jnp.concatenate([before, value, after], axis=dim)
    return value


def wave_vectors(wave_index, domains_x, domains_y):
    scales = jnp.array([two_pi / domains_x, two_pi / domains_y, two_pi], jnp.float32)
    wavevectors = wave_index.astype(jnp.float32) * scales[:, None]
    squared = jnp.sum(wavevectors * wavevectors, axis=0)
    prefactor = 8.0 * math.pi * ewald_scale / (domains_x * domains_y)
    weights = prefactor * jnp.exp(-0.5 * ewald_width * ewald_width * squared) / squared
    return (wavevectors, weights)


def phase_of(absolute, wavevectors):
    return (
        absolute[0][:, None] * wavevectors[0][None, :]
        + absolute[1][:, None] * wavevectors[1][None, :]
        + absolute[2][:, None] * wavevectors[2][None, :]
    )


def structure_terms(absolute, charges, wavevectors):
    stride = math.gcd(wavevectors.shape[1], wave_step)
    block_count = wavevectors.shape[1] // stride

    def one_block(block_index):
        wave_block = lax.dynamic_slice_in_dim(wavevectors, block_index * stride, stride, 1)
        phases = phase_of(absolute, wave_block)
        real_part = jnp.einsum("ak,aq->kq", jnp.cos(phases), charges, precision=highest)
        imag_part = jnp.einsum("ak,aq->kq", jnp.sin(phases), charges, precision=highest)
        return (real_part, imag_part)

    real_part, imag_part = lax.map(one_block, jnp.arange(block_count, dtype=jnp.int32))
    latent = charges.shape[1]
    return (real_part.reshape(-1, latent), imag_part.reshape(-1, latent))


def field_terms(absolute, wavevectors, weights, total_real, total_imag):
    scaled_real = weights[:, None] * total_real
    scaled_imag = weights[:, None] * total_imag
    right_cos = jnp.concatenate(
        [scaled_real] + [-wavevectors[direction][:, None] * scaled_imag for direction in range(3)],
        axis=1,
    )
    right_sin = jnp.concatenate(
        [scaled_imag] + [wavevectors[direction][:, None] * scaled_real for direction in range(3)],
        axis=1,
    )
    stride = math.gcd(wavevectors.shape[1], wave_step)
    block_count = wavevectors.shape[1] // stride

    def accumulate(block_index, running):
        wave_block = lax.dynamic_slice_in_dim(wavevectors, block_index * stride, stride, 1)
        phases = phase_of(absolute, wave_block)
        cos_right = lax.dynamic_slice_in_dim(right_cos, block_index * stride, stride, 0)
        sin_right = lax.dynamic_slice_in_dim(right_sin, block_index * stride, stride, 0)
        running = running + jnp.dot(jnp.cos(phases), cos_right, precision=highest)
        return running + jnp.dot(jnp.sin(phases), sin_right, precision=highest)

    initial = jnp.zeros((absolute.shape[1], right_cos.shape[1]), jnp.float32)
    return lax.fori_loop(0, block_count, accumulate, initial)


def project_pair(feature, weights):
    channels = weights.shape[1]
    row_count = feature.shape[0]
    scalar = jnp.dot(feature[:, :channels], weights[0], preferred_element_type=jnp.float32)
    vector = jnp.dot(
        feature[:, channels:].reshape(row_count * 3, channels),
        weights[1],
        preferred_element_type=jnp.float32,
    )
    return jnp.concatenate([scalar, vector.reshape(row_count, 3 * channels)], axis=1)


def edge_products(
    table_pos, table_up, centre_pos, nbr_rows, nbr_live, coeffs, radial_in, radial_mid, radial_out
):
    atom_count, slot_count = nbr_rows.shape
    edge_count = atom_count * slot_count
    table_size = table_up.shape[0]
    flat_rows = nbr_rows.reshape(edge_count)
    row_onehot = (flat_rows[:, None] == jnp.arange(table_size, dtype=jnp.int32)[None, :]).astype(
        jnp.bfloat16
    )
    picked_pos = jnp.dot(row_onehot.astype(jnp.float32), table_pos.T, precision=highest)
    offset = (picked_pos.T.reshape(3, atom_count, slot_count) - centre_pos[:, :, None]).reshape(
        3, edge_count
    )
    distance = jnp.sqrt(jnp.sum(offset * offset, axis=0))
    scaled_dist = distance / cutoff_radius
    envelope = 1.0 - 28.0 * scaled_dist**6 + 48.0 * scaled_dist**7 - 21.0 * scaled_dist**8
    alive_mask = (
        (jnp.arange(slot_count, dtype=jnp.int32)[None, :] < nbr_live[:, None])
        .astype(jnp.float32)
        .reshape(edge_count)
    )
    basis_count = radial_in.shape[0]
    centres = jnp.arange(basis_count, dtype=jnp.float32) * (cutoff_radius / (basis_count - 1))
    radial_basis = jnp.exp(-basis_sharpness * (distance[:, None] - centres[None, :]) ** 2).astype(
        jnp.bfloat16
    )
    hidden = jax.nn.silu(
        jnp.dot(radial_basis, radial_in, preferred_element_type=jnp.float32)
    ).astype(jnp.bfloat16)
    hidden = jax.nn.silu(jnp.dot(hidden, radial_mid[0], preferred_element_type=jnp.float32)).astype(
        jnp.bfloat16
    )
    hidden = jax.nn.silu(jnp.dot(hidden, radial_mid[1], preferred_element_type=jnp.float32)).astype(
        jnp.bfloat16
    )
    radial = (
        jnp.dot(hidden, radial_out, preferred_element_type=jnp.float32)
        * (envelope * alive_mask)[:, None]
    ).astype(jnp.bfloat16)
    channels = radial.shape[1] // 4
    gathered = jnp.dot(row_onehot, table_up, preferred_element_type=jnp.float32)

    def column_block(source, number):
        return source[:, number * channels : (number + 1) * channels].astype(jnp.float32)

    norm_factor = 1.0 / math.sqrt(slot_count)

    def neighbour_sum(values):
        return jnp.sum(values.reshape(atom_count, slot_count, channels), axis=1) * norm_factor

    up_scalar = column_block(gathered, 0)
    up_vector = [column_block(gathered, 1 + direction) for direction in range(3)]
    along = (
        up_vector[0] * offset[0][:, None]
        + up_vector[1] * offset[1][:, None]
        + up_vector[2] * offset[2][:, None]
    )
    scalar_msg = neighbour_sum(
        column_block(radial, 0) * up_scalar + column_block(radial, 1) * along
    )
    radial_scalar = column_block(radial, 2) * up_scalar
    radial_vector = column_block(radial, 3)
    vector_msg = [
        neighbour_sum(
            radial_scalar * offset[direction][:, None] + radial_vector * up_vector[direction]
        )
        for direction in range(3)
    ]
    square_sum = (
        vector_msg[0] * vector_msg[0]
        + vector_msg[1] * vector_msg[1]
        + vector_msg[2] * vector_msg[2]
    )
    path_weights = [coeffs[:, number * channels : (number + 1) * channels] for number in range(5)]
    scalar_prod = (
        path_weights[0] * scalar_msg
        + path_weights[1] * scalar_msg * scalar_msg
        + path_weights[2] * square_sum
    )
    vector_prod = [
        path_weights[3] * vector_msg[direction]
        + path_weights[4] * scalar_msg * vector_msg[direction]
        for direction in range(3)
    ]
    return jnp.concatenate([scalar_prod] + vector_prod, axis=1).astype(jnp.bfloat16)


def atom_results(
    work_feat,
    products,
    charges,
    efield,
    out_weight,
    skip_weight,
    field_weight,
    read_weight,
    read_vector,
    force_weight,
):
    channels = out_weight.shape[1]
    latent = charges.shape[1]
    mixed_feat = project_pair(products, out_weight) + project_pair(work_feat, skip_weight)
    potential = efield[:, :latent]
    scalars = mixed_feat[:, :channels] + jnp.dot(potential, field_weight, precision=highest)
    readout = jax.nn.silu(
        jnp.dot(scalars.astype(jnp.bfloat16), read_weight, preferred_element_type=jnp.float32)
    )
    energy = jnp.dot(readout, read_vector, precision=highest) + 0.5 * jnp.sum(
        charges * potential, axis=1
    )
    forces = [
        jnp.dot(
            mixed_feat[:, (1 + direction) * channels : (2 + direction) * channels],
            force_weight,
            precision=highest,
        )
        + jnp.sum(charges * efield[:, (1 + direction) * latent : (2 + direction) * latent], axis=1)
        for direction in range(3)
    ]
    return jnp.stack(forces + [energy])


def pick_float(chosen, source):
    return jnp.einsum("ab,bij->aij", chosen, source, precision=highest)


def pick_half(chosen, source):
    return jnp.einsum(
        "ab,bij->aij", chosen.astype(jnp.bfloat16), source, preferred_element_type=jnp.float32
    )


def on_device(
    positions,
    species,
    features,
    move_dest,
    move_slot,
    halo_list,
    neighbours,
    neighbour_count,
    wave_index,
    radial_in,
    radial_mid,
    radial_out,
    up_weight,
    prod_weight,
    out_weight,
    skip_weight,
    charge_weight,
    field_weight,
    read_weight,
    read_vector,
    force_weight,
):
    blocks = move_dest.shape[0]
    atom_count = positions.shape[1]
    block_size = atom_count // blocks
    channels = up_weight.shape[1]
    domains_x = lax.axis_size("gx")
    domains_y = lax.axis_size("yz")
    column = lax.axis_index("yz")
    layer_row = lax.axis_index("gx")
    column_f = column.astype(jnp.float32)
    slot_iota = jnp.arange(blocks, dtype=jnp.int32)
    slot_float = slot_iota.astype(jnp.float32)
    peer_iota = jnp.arange(domains_y, dtype=jnp.int32)
    moving = move_dest != column
    meta_rows = jnp.stack(
        [
            move_slot.astype(jnp.float32) + 1.0,
            slot_float,
            jnp.zeros((blocks,), jnp.float32) + column_f + 1.0,
            move_dest.astype(jnp.float32) + 1.0,
        ],
        axis=1,
    )
    home_geo = jnp.concatenate(
        [
            positions.reshape(3, blocks, block_size).transpose(1, 0, 2),
            species.astype(jnp.bfloat16).reshape(blocks, 1, block_size),
            jnp.broadcast_to(meta_rows[:, :, None], (blocks, 4, block_size)).astype(jnp.bfloat16),
        ],
        axis=1,
    )
    home_feat = features.reshape(blocks, block_size, 4 * channels)
    stay_pick = ((move_slot[None, :] == slot_iota[:, None]) & ~moving[None, :]).astype(jnp.float32)
    send_pick = ((move_dest[None, :] == peer_iota[:, None]) & moving[None, :]).astype(jnp.float32)
    out_geo = pick_half(send_pick, home_geo).astype(jnp.bfloat16)
    out_feat = pick_half(send_pick, home_feat).astype(jnp.bfloat16)
    in_geo, in_feat = (
        lax.all_to_all(out_geo, "yz", split_axis=0, concat_axis=0, tiled=True),
        lax.all_to_all(out_feat, "yz", split_axis=0, concat_axis=0, tiled=True),
    )
    arrive_pick = (
        in_geo[:, 4, 0].astype(jnp.float32)[None, :] == slot_float[:, None] + 1.0
    ).astype(jnp.float32)
    arrive_geo = pick_half(arrive_pick, in_geo)
    arrive_feat = pick_half(arrive_pick, in_feat)
    work_geo = pick_half(stay_pick, home_geo) + arrive_geo
    work_feat = (
        (pick_half(stay_pick, home_feat) + arrive_feat)
        .astype(jnp.bfloat16)
        .reshape(atom_count, 4 * channels)
    )
    work_pos = work_geo[:, :3].transpose(1, 0, 2).reshape(3, atom_count)
    work_species = work_geo[:, 3].reshape(atom_count)
    home_of_slot = work_geo[:, 6, 0] - 1.0
    arrived = home_of_slot != column_f
    list_pick = (halo_list[:, None] == jnp.arange(atom_count, dtype=jnp.int32)[None, :]).astype(
        jnp.float32
    )
    send_pos = jnp.dot(work_pos, list_pick.T, precision=highest).astype(jnp.bfloat16)
    send_feat = jnp.dot(
        list_pick.astype(jnp.bfloat16), work_feat, preferred_element_type=jnp.float32
    ).astype(jnp.bfloat16)
    ext_pos, ext_feat = (
        with_halo(send_pos[None, None], (("gx", 0), ("yz", 1)), 1),
        with_halo(send_feat[None, None], (("gx", 0), ("yz", 1)), 1),
    )
    unit_axes = jnp.eye(3, dtype=jnp.float32)
    ghost_pos = [
        ext_pos[0, 1].astype(jnp.float32) - unit_axes[0][:, None],
        ext_pos[2, 1].astype(jnp.float32) + unit_axes[0][:, None],
        ext_pos[1, 0].astype(jnp.float32) - unit_axes[1][:, None],
        ext_pos[1, 2].astype(jnp.float32) + unit_axes[1][:, None],
    ]
    table_pos = jnp.concatenate([work_pos] + ghost_pos, axis=1)
    table_feat = jnp.concatenate(
        [work_feat, ext_feat[0, 1], ext_feat[2, 1], ext_feat[1, 0], ext_feat[1, 2]], axis=0
    )
    anchor = jnp.stack([layer_row.astype(jnp.float32), column_f, jnp.zeros((), jnp.float32)])
    absolute = work_pos + anchor[:, None]
    charges = jnp.dot(work_feat[:, :channels], charge_weight, preferred_element_type=jnp.float32)
    wavevectors, weights = wave_vectors(wave_index, domains_x, domains_y)
    part_real, part_imag = structure_terms(absolute, charges, wavevectors)
    total_real, total_imag = lax.psum((part_real, part_imag), ("gx", "yz"))
    table_up = project_pair(table_feat, up_weight).astype(jnp.bfloat16)
    onehot = (
        work_species[:, None] == jnp.arange(prod_weight.shape[0], dtype=jnp.float32)[None, :]
    ).astype(jnp.float32)
    coeffs = jnp.dot(onehot, prod_weight, precision=highest)
    block_count = atom_count // atom_step

    def edge_block(pieces):
        return edge_products(
            table_pos,
            table_up,
            pieces[2],
            pieces[0],
            pieces[1],
            pieces[3],
            radial_in,
            radial_mid,
            radial_out,
        )

    products = lax.map(
        edge_block,
        (
            neighbours.reshape(block_count, atom_step, -1),
            neighbour_count.reshape(block_count, atom_step),
            work_pos.reshape(3, block_count, atom_step).transpose(1, 0, 2),
            coeffs.reshape(block_count, atom_step, -1),
        ),
    ).reshape(atom_count, 4 * channels)
    efield = field_terms(absolute, wavevectors, weights, total_real, total_imag)
    results = atom_results(
        work_feat,
        products,
        charges,
        efield,
        out_weight,
        skip_weight,
        field_weight,
        read_weight,
        read_vector,
        force_weight,
    )
    res_blocks = results.reshape(4, blocks, block_size).transpose(1, 0, 2)
    back_pick = (
        (home_of_slot[None, :] == peer_iota.astype(jnp.float32)[:, None]) & arrived[None, :]
    ).astype(jnp.float32)
    sent_back = pick_float(back_pick, res_blocks)
    came_back = lax.all_to_all(sent_back, "yz", split_axis=0, concat_axis=0, tiled=True)
    remote_pick = ((move_dest[:, None] == peer_iota[None, :]) & moving[:, None]).astype(jnp.float32)
    remote = pick_float(remote_pick, came_back)
    home_res = pick_float(stay_pick.T, res_blocks) + remote
    flat_res = home_res.transpose(1, 0, 2).reshape(4, atom_count)
    return (flat_res[:3], flat_res[3])


def solution(mesh):
    in_specs = (
        P(None, ("gx", "yz")),
        P(("gx", "yz")),
        P(("gx", "yz"), None),
        P(("gx", "yz")),
        P(("gx", "yz")),
        P(("gx", "yz")),
        P(("gx", "yz"), None),
        P(("gx", "yz")),
        P(),
        P(),
        P(),
        P(),
        P(),
        P(),
        P(),
        P(),
        P(),
        P(),
        P(),
        P(),
        P(),
    )
    out_specs = (P(None, ("gx", "yz")), P(("gx", "yz")))
    return jax.shard_map(
        on_device, mesh=mesh, in_specs=in_specs, out_specs=out_specs, check_vma=False
    )
```

profile of v0, /device:TPU:0, one launch (start us, length us, event | category | flops | bytes accessed | tf_op | source)
XLA Modules:
  0.0 382.4 jit_solution(8578587456457187002)
XLA Ops:
  12.4 5.2 %all-to-all-start = ((bf16[8,8,128]{2,1,0:T(8,128)(2,1)}), bf16[8,8,128]{2,1,0:T(8,128)(2,1)S(1)}, u32[]{:S(2)}, u32[]{:S(2)}) async-start(bf16[8,8,128]{2,1,0:T(8,128)(2,1)} %copy.64), calls=%async_computation | async-start | bytes 32768 | tf_op jit(solution)/shard_map/all_to_all | solution.py:293
  24.0 4.2 %all-to-all-start.1 = ((bf16[8,128,512]{2,1,0:T(8,128)(2,1)}), bf16[8,128,512]{2,1,0:T(8,128)(2,1)S(1)}, u32[]{:S(2)}, u32[]{:S(2)}) async-start(bf16[8,128,512]{2,1,0:T(8,128)(2,1)} %copy.71), calls=%async_computation.1 | async-start | bytes 2097152 | tf_op jit(solution)/shard_map/all_to_all | solution.py:294
  37.3 5.7 %collective-permute-done.2 = bf16[3,1,3,32]{3,2,1,0:T(4,128)(2,1)S(1)} collective-permute-done((bf16[3,1,3,32]{3,2,1,0:T(4,128)(2,1)S(1)}, bf16[3,1,3,32]{3,2,1,0:T(4,128)(2,1)S(1)}, u32[]{:S(2)}, u32[]{:S(2)}) %collective-permute-start.2) | collective-permute-done | bytes 608 | tf_op jit(solution)/shard_map/ppermute | solution.py:24
  49.9 56.6 %while.37 = (s32[]{:T(128)}, f32[8,512,8]{1,2,0:T(8,128)}, f32[8,512,8]{1,2,0:T(8,128)}, f32[3,256]{1,0:T(4,128)S(1)}, s32[8]{0:T(128)S(1)}, /*index=5*/f32[3,40...) while((s32[]{:T(128)}, f32[8,512,8]{1,2,0:T(8,128)}, ...), condition=%wide.region_9.10_spmd, body=%wide.region_8.9_spmd.sunk | while | flops 26476552 | bytes 87259 | solution.py:58
  51.3 2.9 fusion.239
  54.2 2.9 fusion.238
  58.4 2.9 fusion.239
  65.4 2.9 fusion.239
  72.5 2.9 fusion.239
  79.6 2.9 fusion.239
  86.7 2.9 fusion.239
  93.7 2.9 fusion.239
  96.6 2.9 fusion.238
  100.8 2.9 fusion.239
  103.7 2.9 fusion.238
  110.5 121.8 %all-reduce.3.cloned.1.call-done = (f32[4096,8]{0,1:T(8,128)}, f32[4096,8]{0,1:T(8,128)}) async-done(((f32[4096,8]{0,1:T(8,128)}, f32[4096,8]{0,1:T(8,128)}), (f32[4096,8]{0,1:T(8,128)}, f32[4096,8]{0,1:T(8,128)})) %all-reduce.3.cloned.1.call-update) | async-done | bytes 262160 | tf_op jit(solution)/shard_map/psum | solution.py:338
  233.5 54.9 %while.38 = (s32[]{:T(128)}, f32[256,32]{0,1:T(8,128)S(1)}, f32[3,256]{1,0:T(4,128)S(1)}, f32[3,4096]{1,0:T(4,128)S(1)}, f32[4096,32]{0,1:T(8,128)S(1)}, /*index...) while((s32[]{:T(128)}, f32[256,32]{0,1:T(8,128)S(1)}, ...), condition=%wide.region_13.14_spmd.clone, body=%wide.region_12.13_spmd.clone.sunk | while | flops 101998600 | bytes 299225 | solution.py:86
  234.2 3.1 convolution_add_fusion.8
  237.2 3.1 convolution_add_fusion.9
  241.0 3.1 convolution_add_fusion.8
  244.1 3.1 convolution_add_fusion.9
  247.9 3.1 convolution_add_fusion.8
  251.0 3.1 convolution_add_fusion.9
  254.8 3.1 convolution_add_fusion.8
  257.8 3.1 convolution_add_fusion.9
  261.6 3.1 convolution_add_fusion.8
  264.7 3.1 convolution_add_fusion.9
  268.5 3.1 convolution_add_fusion.8
  271.6 3.1 convolution_add_fusion.9
  275.4 3.1 convolution_add_fusion.8
  278.4 3.1 convolution_add_fusion.9
  282.2 3.1 convolution_add_fusion.8
  285.3 3.1 convolution_add_fusion.9
  291.8 70.9 %while.36 = (s32[]{:T(128)}, bf16[4,64,512]{2,1,0:T(8,128)(2,1)S(1)}, f32[4,64,640]{2,1,0:T(8,128)S(1)}, s32[4,64,64]{2,1,0:T(8,128)S(1)}, f32[3,384]{1,0:T(4,12...) while((s32[]{:T(128)}, ...), condition=%wide.region_6.7_spmd, body=%wide.region_0.6_spmd.sunk | while | flops 2032549888 | bytes 45476804 | solution.py:359
  293.0 3.1 multiply_reduce_fusion.7
  298.7 4.6 %multiply_convert_fusion.13 = bf16[4096,512]{1,0:T(8,128)(2,1)} fusion(bf16[64,512]{1,0:T(8,128)(2,1)S(1)} %get-tuple-element.587, f32[4096]{0:T(1024)S(1)} %get-tuple-element.517, bf16[4096,64]{0,1:T(8,128)(2,1)} %multiply_convert_fusion.12, bf16[2,64,64]{2,1,0:T(8,128)(2,1)S(1)} %get-tuple-element.586), kind=kOutput, calls=%fused_computation.clone.1 | convolution fusion | flops 307494912 | bytes 4816896 | tf_op jit(solution)/shard_map/while/body/eval_jaxpr/dot_general | solution.py:138
  306.1 3.4 bitcast_reduce_fusion.5
  310.6 3.1 multiply_reduce_fusion.7
  316.3 4.6 %multiply_convert_fusion.13 = bf16[4096,512]{1,0:T(8,128)(2,1)} fusion(bf16[64,512]{1,0:T(8,128)(2,1)S(1)} %get-tuple-element.587, f32[4096]{0:T(1024)S(1)} %get-tuple-element.517, bf16[4096,64]{0,1:T(8,128)(2,1)} %multiply_convert_fusion.12, bf16[2,64,64]{2,1,0:T(8,128)(2,1)S(1)} %get-tuple-element.586), kind=kOutput, calls=%fused_computation.clone.1 | convolution fusion | flops 307494912 | bytes 4816896 | tf_op jit(solution)/shard_map/while/body/eval_jaxpr/dot_general | solution.py:138
  323.8 3.4 bitcast_reduce_fusion.5
  328.3 3.1 multiply_reduce_fusion.7
  334.0 4.6 %multiply_convert_fusion.13 = bf16[4096,512]{1,0:T(8,128)(2,1)} fusion(bf16[64,512]{1,0:T(8,128)(2,1)S(1)} %get-tuple-element.587, f32[4096]{0:T(1024)S(1)} %get-tuple-element.517, bf16[4096,64]{0,1:T(8,128)(2,1)} %multiply_convert_fusion.12, bf16[2,64,64]{2,1,0:T(8,128)(2,1)S(1)} %get-tuple-element.586), kind=kOutput, calls=%fused_computation.clone.1 | convolution fusion | flops 307494912 | bytes 4816896 | tf_op jit(solution)/shard_map/while/body/eval_jaxpr/dot_general | solution.py:138
  341.5 3.4 bitcast_reduce_fusion.5
  346.0 3.1 multiply_reduce_fusion.7
  351.7 4.6 %multiply_convert_fusion.13 = bf16[4096,512]{1,0:T(8,128)(2,1)} fusion(bf16[64,512]{1,0:T(8,128)(2,1)S(1)} %get-tuple-element.587, f32[4096]{0:T(1024)S(1)} %get-tuple-element.517, bf16[4096,64]{0,1:T(8,128)(2,1)} %multiply_convert_fusion.12, bf16[2,64,64]{2,1,0:T(8,128)(2,1)S(1)} %get-tuple-element.586), kind=kOutput, calls=%fused_computation.clone.1 | convolution fusion | flops 307494912 | bytes 4816896 | tf_op jit(solution)/shard_map/while/body/eval_jaxpr/dot_general | solution.py:138
  359.1 3.4 bitcast_reduce_fusion.5
  365.8 3.6 all-to-all-start.2
  369.6 4.5 %all-to-all-done.2 = f32[8,4,128]{2,1,0:T(4,128)S(1)} async-done(((f32[8,4,128]{2,1,0:T(4,128)}), f32[8,4,128]{2,1,0:T(4,128)S(1)}, u32[]{:S(2)}, u32[]{:S(2)}) %all-to-all-start.2) | async-done | bytes 16416 | tf_op jit(solution)/shard_map/all_to_all | solution.py:386
  (320 shorter events, 91.1 us)
Async XLA Ops:
  7.2 11.3 %copy-start = (bf16[256,512]{1,0:T(8,128)(2,1)S(1)}, bf16[256,512]{1,0:T(8,128)(2,1)}, u32[]{:S(2)}) copy-start(bf16[256,512]{1,0:T(8,128)(2,1)} %param.30) | copy-start | bytes 786436
  7.2 14.4 %copy-start.18 = (f32[3]{0:T(128)S(1)}, f32[3]{0:T(128)}, u32[]{:S(2)}) copy-start(f32[3]{0:T(128)} %constant.114.clone) | copy-start | bytes 40
  7.2 14.4 %copy-start.6 = (s32[3,4096]{1,0:T(4,128)S(1)}, s32[3,4096]{1,0:T(4,128)}, u32[]{:S(2)}) copy-start(s32[3,4096]{1,0:T(4,128)} %param.36) | copy-start | bytes 147460
  8.6 14.6 %copy-start.14 = (pred[2]{0:T(512)(128)(4,1)}, pred[2]{0:T(512)(128)(4,1)S(1)}, u32[]{:S(2)}) copy-start(pred[2]{0:T(512)(128)(4,1)S(1)} %get-tuple-element.307) | copy-start | bytes 10
  8.6 14.6 %copy-start.19 = (pred[2]{0:T(512)(128)(4,1)}, pred[2]{0:T(512)(128)(4,1)S(1)}, u32[]{:S(2)}) copy-start(pred[2]{0:T(512)(128)(4,1)S(1)} %get-tuple-element.306) | copy-start | bytes 10
  12.4 11.6 %all-to-all-start = ((bf16[8,8,128]{2,1,0:T(8,128)(2,1)}), bf16[8,8,128]{2,1,0:T(8,128)(2,1)S(1)}, u32[]{:S(2)}, u32[]{:S(2)}) async-start(bf16[8,8,128]{2,1,0:T(8,128)(2,1)} %copy.64), calls=%async_computation | async-start | bytes 32768 | tf_op jit(solution)/shard_map/all_to_all | solution.py:293
  18.5 4.7 %copy-start.2 = (s32[256,64]{0,1:T(8,128)S(1)}, s32[256,64]{0,1:T(8,128)}, u32[]{:S(2)}) copy-start(s32[256,64]{0,1:T(8,128)} %param.34) | copy-start | bytes 196612
  19.8 3.6 copy-start.16
  21.9 6.7 %copy-start.17 = (s32[32]{0:T(128)S(1)}, s32[32]{0:T(128)}, u32[]{:S(2)}) copy-start(s32[32]{0:T(128)} %param.33) | copy-start | bytes 388
  21.9 11.5 %copy-start.7 = (f32[6,640]{1,0:T(8,128)S(1)}, f32[6,640]{1,0:T(8,128)}, u32[]{:S(2)}) copy-start(f32[6,640]{1,0:T(8,128)} %param.41) | copy-start | bytes 46084
  24.0 19.8 %all-to-all-start.1 = ((bf16[8,128,512]{2,1,0:T(8,128)(2,1)}), bf16[8,128,512]{2,1,0:T(8,128)(2,1)S(1)}, u32[]{:S(2)}, u32[]{:S(2)}) async-start(bf16[8,128,512]{2,1,0:T(8,128)(2,1)} %copy.71), calls=%async_computation.1 | async-start | bytes 2097152 | tf_op jit(solution)/shard_map/all_to_all | solution.py:294
  28.2 21.6 %copy-start.23 = (bf16[128,8]{0,1:T(8,128)(2,1)S(1)}, bf16[128,8]{0,1:T(8,128)(2,1)}, u32[]{:S(2)}) copy-start(bf16[128,8]{0,1:T(8,128)(2,1)} %param.44) | copy-start | bytes 6148
  28.2 204.1 %all-reduce.3.cloned.1.call-start = ((), (), s32[]{:S(2)}) async-start(), calls=%async_computation.3 | async-start | bytes 524288 | tf_op jit(solution)/shard_map/psum | solution.py:338
  28.8 5.8 %collective-permute-start = (bf16[1,1,3,32]{3,2,1,0:T(4,128)(2,1)S(1)}, bf16[1,1,3,32]{3,2,1,0:T(4,128)(2,1)S(1)}, u32[]{:S(2)}, u32[]{:S(2)}) collective-permute-start(bf16[1,1,3,32]{3,2,1,0:T(4,128)(2,1)S(1)} %fusion.86), channel_id=1, source_target_pairs={{0,8},{8,16},{16,24},{24,0},{1,9},{9,17},{17,25},{25,1},{2,10},{10... | collective-permute-start | bytes 584 | tf_op jit(solution)/shard_map/ppermute | solution.py:24
  30.3 4.2 %collective-permute-start.1 = (bf16[1,1,3,32]{3,2,1,0:T(4,128)(2,1)S(1)}, bf16[1,1,3,32]{3,2,1,0:T(4,128)(2,1)S(1)}, u32[]{:S(2)}, u32[]{:S(2)}) collective-permute-start(bf16[1,1,3,32]{3,2,1,0:T(4,128)(2,1)S(1)} %fusion.86), channel_id=1, source_target_pairs={{8,0},{16,8},{24,16},{0,24},{9,1},{17,9},{25,17},{1,25},{10,2},{18... | collective-permute-start | bytes 584 | tf_op jit(solution)/shard_map/ppermute | solution.py:25
  32.7 13.0 %copy-start.27 = (f32[2]{0:T(128)}, f32[2]{0:T(128)S(1)}, u32[]{:S(2)}) copy-start(f32[2]{0:T(128)S(1)} %fusion.147) | copy-start | bytes 28
  34.6 8.5 %collective-permute-start.2 = (bf16[3,1,3,32]{3,2,1,0:T(4,128)(2,1)S(1)}, bf16[3,1,3,32]{3,2,1,0:T(4,128)(2,1)S(1)}, u32[]{:S(2)}, u32[]{:S(2)}) collective-permute-start(bf16[3,1,3,32]{3,2,1,0:T(4,128)(2,1)S(1)} %pad_maximum_fusion.5), channel_id=1, source_target_pairs={{0,1},{1,2},{2,3},{3,4},{4,5},{5,6},{6,7},{7,0},{8,9},{9,10},{10,1... | collective-permute-start | bytes 1736 | tf_op jit(solution)/shard_map/ppermute | solution.py:24
  34.6 8.4 %collective-permute-start.3 = (bf16[3,1,3,32]{3,2,1,0:T(4,128)(2,1)S(1)}, bf16[3,1,3,32]{3,2,1,0:T(4,128)(2,1)S(1)}, u32[]{:S(2)}, u32[]{:S(2)}) collective-permute-start(bf16[3,1,3,32]{3,2,1,0:T(4,128)(2,1)S(1)} %pad_maximum_fusion.5), channel_id=1, source_target_pairs={{1,0},{2,1},{3,2},{4,3},{5,4},{6,5},{7,6},{0,7},{9,8},{10,9},{11,1... | collective-permute-start | bytes 1736 | tf_op jit(solution)/shard_map/ppermute | solution.py:25
  45.9 61.9 %collective-permute-start.4 = (bf16[1,1,32,512]{3,2,1,0:T(8,128)(2,1)S(1)}, bf16[1,1,32,512]{3,2,1,0:T(8,128)(2,1)S(1)}, u32[]{:S(2)}, u32[]{:S(2)}) collective-permute-start(bf16[1,1,32,512]{3,2,1,0:T(8,128)(2,1)S(1)} %fusion.84), channel_id=1, source_target_pairs={{0,8},{8,16},{16,24},{24,0},{1,9},{9,17},{17,25},{25,1},{2,10},{10... | collective-permute-start | bytes 98312 | tf_op jit(solution)/shard_map/ppermute | solution.py:24
  47.5 60.3 %collective-permute-start.5 = (bf16[1,1,32,512]{3,2,1,0:T(8,128)(2,1)S(1)}, bf16[1,1,32,512]{3,2,1,0:T(8,128)(2,1)S(1)}, u32[]{:S(2)}, u32[]{:S(2)}) collective-permute-start(bf16[1,1,32,512]{3,2,1,0:T(8,128)(2,1)S(1)} %fusion.84), channel_id=1, source_target_pairs={{8,0},{16,8},{24,16},{0,24},{9,1},{17,9},{25,17},{1,25},{10,2},{18... | collective-permute-start | bytes 98312 | tf_op jit(solution)/shard_map/ppermute | solution.py:25
  49.9 57.3 %copy-start.3 = (bf16[2,128,128]{2,1,0:T(8,128)(2,1)S(1)}, bf16[2,128,128]{2,1,0:T(8,128)(2,1)}, u32[]{:S(2)}) copy-start(bf16[2,128,128]{2,1,0:T(8,128)(2,1)} %param.43) | copy-start | bytes 196612
  106.6 0.6 copy-start.8
  107.8 181.4 %collective-permute-start.6 = (bf16[3,1,32,512]{3,2,1,0:T(8,128)(2,1)S(1)}, bf16[3,1,32,512]{3,2,1,0:T(8,128)(2,1)}, u32[]{:S(2)}, u32[]{:S(2)}) collective-permute-start(bf16[3,1,32,512]{3,2,1,0:T(8,128)(2,1)S(1)} %pad_maximum_fusion.3), channel_id=1, source_target_pairs={{0,1},{1,2},{2,3},{3,4},{4,5},{5,6},{6,7},{7,0},{8,9},{9,10},{10,1... | collective-permute-start | bytes 294920 | tf_op jit(solution)/shard_map/ppermute | solution.py:24
  107.9 182.1 %collective-permute-start.7 = (bf16[3,1,32,512]{3,2,1,0:T(8,128)(2,1)S(1)}, bf16[3,1,32,512]{3,2,1,0:T(8,128)(2,1)}, u32[]{:S(2)}, u32[]{:S(2)}) collective-permute-start(bf16[3,1,32,512]{3,2,1,0:T(8,128)(2,1)S(1)} %pad_maximum_fusion.3), channel_id=1, source_target_pairs={{1,0},{2,1},{3,2},{4,3},{5,4},{6,5},{7,6},{0,7},{9,8},{10,9},{11,1... | collective-permute-start | bytes 294920 | tf_op jit(solution)/shard_map/ppermute | solution.py:25
  233.5 57.4 %copy-start.4 = (bf16[2,128,128]{2,1,0:T(8,128)(2,1)S(1)}, bf16[2,128,128]{2,1,0:T(8,128)(2,1)}, u32[]{:S(2)}) copy-start(bf16[2,128,128]{2,1,0:T(8,128)(2,1)} %param.40) | copy-start | bytes 196612
  288.4 3.3 copy-start.9
  288.4 3.3 copy-start.21
  288.4 3.3 copy-start.22
  288.4 3.3 copy-start.24
  291.7 71.1 %copy-start.5 = (bf16[2,128,128]{2,1,0:T(8,128)(2,1)S(1)}, bf16[2,128,128]{2,1,0:T(8,128)(2,1)}, u32[]{:S(2)}) copy-start(bf16[2,128,128]{2,1,0:T(8,128)(2,1)} %param.42) | copy-start | bytes 196612
  303.7 2.4 copy-start.1
  321.4 2.4 copy-start.1
  339.0 2.4 copy-start.1
  356.7 2.4 copy-start.1
  362.6 0.8 copy-start.10
  362.7 1.4 copy-start.11
  362.7 1.9 copy-start.12
  362.7 2.0 copy-start.25
  362.8 2.0 copy-start.28
  362.8 2.0 copy-start.29
  362.9 2.0 copy-start.30
  362.9 6.6 %copy-start.20 = (pred[2]{0:T(512)(128)(4,1)S(1)}, pred[2]{0:T(512)(128)(4,1)}, u32[]{:S(2)}) copy-start(pred[2]{0:T(512)(128)(4,1)} %copy-done.19) | copy-start | bytes 10
  362.9 6.6 %copy-start.26 = (s32[2]{0:T(128)S(1)}, s32[2]{0:T(128)}, u32[]{:S(2)}) copy-start(s32[2]{0:T(128)} %param.32) | copy-start | bytes 28
  363.0 11.2 %copy-start.13 = (s32[2]{0:T(128)S(1)}, s32[2]{0:T(128)}, u32[]{:S(2)}) copy-start(s32[2]{0:T(128)} %param.31) | copy-start | bytes 28
  363.0 11.1 %copy-start.15 = (pred[2]{0:T(512)(128)(4,1)S(1)}, pred[2]{0:T(512)(128)(4,1)}, u32[]{:S(2)}) copy-start(pred[2]{0:T(512)(128)(4,1)} %copy-done.14) | copy-start | bytes 10
  365.8 8.4 %all-to-all-start.2 = ((f32[8,4,128]{2,1,0:T(4,128)}), f32[8,4,128]{2,1,0:T(4,128)S(1)}, u32[]{:S(2)}, u32[]{:S(2)}) async-start(f32[8,4,128]{2,1,0:T(4,128)} %copy.79), calls=%async_computation.2 | async-start | bytes 32768 | tf_op jit(solution)/shard_map/all_to_all | solution.py:386
Sparse Core Ops, SparseCore 0:
  107.9 124.3 all-reduce.2
where the time goes:
time: 384 us; the launch traced here: 382 us
  matrix products  152 us (40%)
  waiting for transfers between devices  132 us (34%)
  local copies, waits for them, and re-layouts  29 us (8%)
  starting transfers between devices  26.1 us (7%)
  other arithmetic  22 us (6%)
  between operations  14.7 us (4%)
  loops' own time  6.29 us (2%)
    psum x1, waiting for transfers between devices, on_device(): total_real, total_imag = lax.psum((part_real, part_imag), ('gx', 'yz'))  122 us
    dot_general x8, matrix products, accumulate(): return running + jnp.dot(jnp.sin(phases), sin_right, precision=highest)  24.7 us
    dot_general x8, matrix products, accumulate(): running = running + jnp.dot(jnp.cos(phases), cos_right, precision=highest)  24.5 us
    dot_general x8, matrix products, one_block(): jnp.einsum('ak,aq->kq', jnp.sin(phases), charges, precision=highest)  23.1 us
    dot_general x8, matrix products, one_block(): jnp.einsum('ak,aq->kq', jnp.cos(phases), charges, precision=highest)  22.9 us
    dot_general x4, matrix products, edge_products(): jnp.dot(hidden, radial_out, preferred_element_type=jnp.float32)  18.3 us
    reduce_sum x4, other arithmetic, neighbour_sum(): jnp.sum(values.reshape(atom_count, slot_count, channels), axis=1)  13.6 us
    dot_general x4, matrix products, edge_products(): jnp.dot(row_onehot.astype(jnp.float32), table_pos.T, precision=highest)  12.4 us
  transfers between devices with their start and end apart: 12, of which 3 were waited for; matrix products, arithmetic and copies ran while one was open for 31% of the time, Pallas kernels for 0%

commit v1 on v0

--- a/solution.py
+++ b/solution.py
@@ -335,7 +335,7 @@
     charges = jnp.dot(work_feat[:, :channels], charge_weight, preferred_element_type=jnp.float32)
     wavevectors, weights = wave_vectors(wave_index, domains_x, domains_y)
     part_real, part_imag = structure_terms(absolute, charges, wavevectors)
-    total_real, total_imag = lax.psum((part_real, part_imag), ("gx", "yz"))
+    total_real, total_imag = lax.psum(lax.psum((part_real, part_imag), "yz"), "gx")
     table_up = project_pair(table_feat, up_weight).astype(jnp.bfloat16)
     onehot = (
         work_species[:, None] == jnp.arange(prod_weight.shape[0], dtype=jnp.float32)[None, :]

time: 384 us -> 275 us (0.72)
  waiting for transfers between devices: 132 us -> 60.9 us
  matrix products: 152 us -> 131 us
  local copies, waits for them, and re-layouts: 29 us -> 15.1 us
    psum x1 -> x2, waiting for transfers between devices: 122 us -> 48.9 us  [the longest x1 48.9 us: on_device(): lax.psum((part_real, part_imag), 'yz')]
    dot_general x8, matrix products: 24.7 us -> 19.2 us  [accumulate(): return running + jnp.dot(jnp.sin(phases), sin_right, precision=highest)]
    dot_general x8, matrix products: 24.5 us -> 19.1 us  [accumulate(): running = running + jnp.dot(jnp.cos(phases), cos_right, precision=highest)]
    dot_general x4, matrix products: 18.3 us -> 13.3 us  [edge_products(): jnp.dot(hidden, radial_out, preferred_element_type=jnp.float32)]
    slice x16, local copies, waits for them, and re-layouts: 4.75 us -> 0.07 us  [phase_of(): absolute[0][:, None] * wavevectors[0][None, :]]
  transfers between devices with their start and end apart: 12 -> 13, of which waited for: 3 -> 6; matrix products, arithmetic and copies ran while one was open for 31% -> 43% of each run, Pallas kernels for 0% -> 0%
where the time goes in v1:
time: 275 us; the launch traced here: 274 us
  matrix products  131 us (48%)
  waiting for transfers between devices  60.9 us (22%)
  starting transfers between devices  25.7 us (9%)
  other arithmetic  20.2 us (7%)
  local copies, waits for them, and re-layouts  15.1 us (5%)
  between operations  14.7 us (5%)
  loops' own time  6.33 us (2%)
    psum x1, waiting for transfers between devices, on_device(): lax.psum((part_real, part_imag), 'yz')  48.9 us
    dot_general x8, matrix products, one_block(): jnp.einsum('ak,aq->kq', jnp.sin(phases), charges, precision=highest)  23.1 us
    dot_general x8, matrix products, one_block(): jnp.einsum('ak,aq->kq', jnp.cos(phases), charges, precision=highest)  22.9 us
    dot_general x8, matrix products, accumulate(): return running + jnp.dot(jnp.sin(phases), sin_right, precision=highest)  19.2 us
    dot_general x8, matrix products, accumulate(): running = running + jnp.dot(jnp.cos(phases), cos_right, precision=highest)  19.1 us
    reduce_sum x4, other arithmetic, neighbour_sum(): jnp.sum(values.reshape(atom_count, slot_count, channels), axis=1)  13.5 us
    dot_general x4, matrix products, edge_products(): jnp.dot(hidden, radial_out, preferred_element_type=jnp.float32)  13.3 us
    dot_general x4, matrix products, edge_products(): jnp.dot(row_onehot.astype(jnp.float32), table_pos.T, precision=highest)  12.4 us
  transfers between devices with their start and end apart: 13, of which 6 were waited for; matrix products, arithmetic and copies ran while one was open for 43% of the time, Pallas kernels for 0%

profile of v1, /device:TPU:0, one launch (start us, length us, event | category | flops | bytes accessed | tf_op | source)
XLA Modules:
  0.0 274.0 jit_solution(7925408371000439181)
XLA Ops:
  12.4 5.2 %all-to-all-start = ((bf16[8,8,128]{2,1,0:T(8,128)(2,1)}), bf16[8,8,128]{2,1,0:T(8,128)(2,1)S(1)}, u32[]{:S(2)}, u32[]{:S(2)}) async-start(bf16[8,8,128]{2,1,0:T(8,128)(2,1)} %copy.64), calls=%async_computation | async-start | bytes 32768 | tf_op jit(solution)/shard_map/all_to_all | solution.py:293
  22.3 4.0 %all-to-all-start.1 = ((bf16[8,128,512]{2,1,0:T(8,128)(2,1)}), bf16[8,128,512]{2,1,0:T(8,128)(2,1)S(1)}, u32[]{:S(2)}, u32[]{:S(2)}) async-start(bf16[8,128,512]{2,1,0:T(8,128)(2,1)} %copy.71), calls=%async_computation.1 | async-start | bytes 2097152 | tf_op jit(solution)/shard_map/all_to_all | solution.py:294
  32.4 2.6 collective-permute-start.3
  35.1 6.1 %collective-permute-done.2 = bf16[3,1,3,32]{3,2,1,0:T(4,128)(2,1)S(1)} collective-permute-done((bf16[3,1,3,32]{3,2,1,0:T(4,128)(2,1)S(1)}, bf16[3,1,3,32]{3,2,1,0:T(4,128)(2,1)S(1)}, u32[]{:S(2)}, u32[]{:S(2)}) %collective-permute-start.2) | collective-permute-done | bytes 608 | tf_op jit(solution)/shard_map/ppermute | solution.py:24
  46.8 56.6 %while.37 = (s32[]{:T(128)}, f32[8,512,8]{1,2,0:T(8,128)}, f32[8,512,8]{1,2,0:T(8,128)}, f32[3,256]{1,0:T(4,128)S(1)}, s32[8]{0:T(128)S(1)}, /*index=5*/f32[3,40...) while((s32[]{:T(128)}, f32[8,512,8]{1,2,0:T(8,128)}, ...), condition=%wide.region_9.10_spmd, body=%wide.region_8.9_spmd.sunk | while | flops 26476552 | bytes 87259 | solution.py:58
  48.2 2.9 %fusion.239 = f32[8,512,8]{1,2,0:T(8,128)} fusion(f32[8,512,8]{1,2,0:T(8,128)} %get-tuple-element.608, s32[]{:T(128)} %get-tuple-element.606, f32[256,8]{0,1:T(8,128)S(1)} %get-tuple-element.625, f32[512]{0:T(512)S(1)} %bitcast.308, f32[256]{0:T(256)S(1)} %bitcast.319, f32[512]{0:T(512)S(1)} %bitcast.306, f32[256]{0:T(256)S(1)} %bitcast.321, ...), kind=kOutput, calls=%fused_computation.74.clone.1 | convolution fusion | flops 13238272 | bytes 34304 | tf_op jit(solution)/shard_map/while/body/eval_jaxpr/ak,aq->kq/dot_general | solution.py:55
  51.1 2.9 %fusion.238 = f32[8,512,8]{1,2,0:T(8,128)} fusion(f32[8,512,8]{1,2,0:T(8,128)} %get-tuple-element.607, s32[]{:T(128)} %get-tuple-element.606, f32[256,8]{0,1:T(8,128)S(1)} %get-tuple-element.625, f32[512]{0:T(512)S(1)} %bitcast.309, f32[256]{0:T(256)S(1)} %bitcast.320, f32[512]{0:T(512)S(1)} %bitcast.307, f32[256]{0:T(256)S(1)} %bitcast.322, ...), kind=kOutput, calls=%fused_computation.76.clone.1 | convolution fusion | flops 13238272 | bytes 34304 | tf_op jit(solution)/shard_map/while/body/eval_jaxpr/ak,aq->kq/dot_general | solution.py:54
  55.2 2.9 %fusion.239 = f32[8,512,8]{1,2,0:T(8,128)} fusion(f32[8,512,8]{1,2,0:T(8,128)} %get-tuple-element.608, s32[]{:T(128)} %get-tuple-element.606, f32[256,8]{0,1:T(8,128)S(1)} %get-tuple-element.625, f32[512]{0:T(512)S(1)} %bitcast.308, f32[256]{0:T(256)S(1)} %bitcast.319, f32[512]{0:T(512)S(1)} %bitcast.306, f32[256]{0:T(256)S(1)} %bitcast.321, ...), kind=kOutput, calls=%fused_computation.74.clone.1 | convolution fusion | flops 13238272 | bytes 34304 | tf_op jit(solution)/shard_map/while/body/eval_jaxpr/ak,aq->kq/dot_general | solution.py:55
  58.1 2.9 %fusion.238 = f32[8,512,8]{1,2,0:T(8,128)} fusion(f32[8,512,8]{1,2,0:T(8,128)} %get-tuple-element.607, s32[]{:T(128)} %get-tuple-element.606, f32[256,8]{0,1:T(8,128)S(1)} %get-tuple-element.625, f32[512]{0:T(512)S(1)} %bitcast.309, f32[256]{0:T(256)S(1)} %bitcast.320, f32[512]{0:T(512)S(1)} %bitcast.307, f32[256]{0:T(256)S(1)} %bitcast.322, ...), kind=kOutput, calls=%fused_computation.76.clone.1 | convolution fusion | flops 13238272 | bytes 34304 | tf_op jit(solution)/shard_map/while/body/eval_jaxpr/ak,aq->kq/dot_general | solution.py:54
  62.3 2.9 %fusion.239 = f32[8,512,8]{1,2,0:T(8,128)} fusion(f32[8,512,8]{1,2,0:T(8,128)} %get-tuple-element.608, s32[]{:T(128)} %get-tuple-element.606, f32[256,8]{0,1:T(8,128)S(1)} %get-tuple-element.625, f32[512]{0:T(512)S(1)} %bitcast.308, f32[256]{0:T(256)S(1)} %bitcast.319, f32[512]{0:T(512)S(1)} %bitcast.306, f32[256]{0:T(256)S(1)} %bitcast.321, ...), kind=kOutput, calls=%fused_computation.74.clone.1 | convolution fusion | flops 13238272 | bytes 34304 | tf_op jit(solution)/shard_map/while/body/eval_jaxpr/ak,aq->kq/dot_general | solution.py:55
  65.2 2.9 %fusion.238 = f32[8,512,8]{1,2,0:T(8,128)} fusion(f32[8,512,8]{1,2,0:T(8,128)} %get-tuple-element.607, s32[]{:T(128)} %get-tuple-element.606, f32[256,8]{0,1:T(8,128)S(1)} %get-tuple-element.625, f32[512]{0:T(512)S(1)} %bitcast.309, f32[256]{0:T(256)S(1)} %bitcast.320, f32[512]{0:T(512)S(1)} %bitcast.307, f32[256]{0:T(256)S(1)} %bitcast.322, ...), kind=kOutput, calls=%fused_computation.76.clone.1 | convolution fusion | flops 13238272 | bytes 34304 | tf_op jit(solution)/shard_map/while/body/eval_jaxpr/ak,aq->kq/dot_general | solution.py:54
  69.4 2.9 %fusion.239 = f32[8,512,8]{1,2,0:T(8,128)} fusion(f32[8,512,8]{1,2,0:T(8,128)} %get-tuple-element.608, s32[]{:T(128)} %get-tuple-element.606, f32[256,8]{0,1:T(8,128)S(1)} %get-tuple-element.625, f32[512]{0:T(512)S(1)} %bitcast.308, f32[256]{0:T(256)S(1)} %bitcast.319, f32[512]{0:T(512)S(1)} %bitcast.306, f32[256]{0:T(256)S(1)} %bitcast.321, ...), kind=kOutput, calls=%fused_computation.74.clone.1 | convolution fusion | flops 13238272 | bytes 34304 | tf_op jit(solution)/shard_map/while/body/eval_jaxpr/ak,aq->kq/dot_general | solution.py:55
  72.3 2.9 %fusion.238 = f32[8,512,8]{1,2,0:T(8,128)} fusion(f32[8,512,8]{1,2,0:T(8,128)} %get-tuple-element.607, s32[]{:T(128)} %get-tuple-element.606, f32[256,8]{0,1:T(8,128)S(1)} %get-tuple-element.625, f32[512]{0:T(512)S(1)} %bitcast.309, f32[256]{0:T(256)S(1)} %bitcast.320, f32[512]{0:T(512)S(1)} %bitcast.307, f32[256]{0:T(256)S(1)} %bitcast.322, ...), kind=kOutput, calls=%fused_computation.76.clone.1 | convolution fusion | flops 13238272 | bytes 34304 | tf_op jit(solution)/shard_map/while/body/eval_jaxpr/ak,aq->kq/dot_general | solution.py:54
  76.5 2.9 %fusion.239 = f32[8,512,8]{1,2,0:T(8,128)} fusion(f32[8,512,8]{1,2,0:T(8,128)} %get-tuple-element.608, s32[]{:T(128)} %get-tuple-element.606, f32[256,8]{0,1:T(8,128)S(1)} %get-tuple-element.625, f32[512]{0:T(512)S(1)} %bitcast.308, f32[256]{0:T(256)S(1)} %bitcast.319, f32[512]{0:T(512)S(1)} %bitcast.306, f32[256]{0:T(256)S(1)} %bitcast.321, ...), kind=kOutput, calls=%fused_computation.74.clone.1 | convolution fusion | flops 13238272 | bytes 34304 | tf_op jit(solution)/shard_map/while/body/eval_jaxpr/ak,aq->kq/dot_general | solution.py:55
  79.4 2.9 %fusion.238 = f32[8,512,8]{1,2,0:T(8,128)} fusion(f32[8,512,8]{1,2,0:T(8,128)} %get-tuple-element.607, s32[]{:T(128)} %get-tuple-element.606, f32[256,8]{0,1:T(8,128)S(1)} %get-tuple-element.625, f32[512]{0:T(512)S(1)} %bitcast.309, f32[256]{0:T(256)S(1)} %bitcast.320, f32[512]{0:T(512)S(1)} %bitcast.307, f32[256]{0:T(256)S(1)} %bitcast.322, ...), kind=kOutput, calls=%fused_computation.76.clone.1 | convolution fusion | flops 13238272 | bytes 34304 | tf_op jit(solution)/shard_map/while/body/eval_jaxpr/ak,aq->kq/dot_general | solution.py:54
  83.6 2.9 %fusion.239 = f32[8,512,8]{1,2,0:T(8,128)} fusion(f32[8,512,8]{1,2,0:T(8,128)} %get-tuple-element.608, s32[]{:T(128)} %get-tuple-element.606, f32[256,8]{0,1:T(8,128)S(1)} %get-tuple-element.625, f32[512]{0:T(512)S(1)} %bitcast.308, f32[256]{0:T(256)S(1)} %bitcast.319, f32[512]{0:T(512)S(1)} %bitcast.306, f32[256]{0:T(256)S(1)} %bitcast.321, ...), kind=kOutput, calls=%fused_computation.74.clone.1 | convolution fusion | flops 13238272 | bytes 34304 | tf_op jit(solution)/shard_map/while/body/eval_jaxpr/ak,aq->kq/dot_general | solution.py:55
  86.4 2.9 %fusion.238 = f32[8,512,8]{1,2,0:T(8,128)} fusion(f32[8,512,8]{1,2,0:T(8,128)} %get-tuple-element.607, s32[]{:T(128)} %get-tuple-element.606, f32[256,8]{0,1:T(8,128)S(1)} %get-tuple-element.625, f32[512]{0:T(512)S(1)} %bitcast.309, f32[256]{0:T(256)S(1)} %bitcast.320, f32[512]{0:T(512)S(1)} %bitcast.307, f32[256]{0:T(256)S(1)} %bitcast.322, ...), kind=kOutput, calls=%fused_computation.76.clone.1 | convolution fusion | flops 13238272 | bytes 34304 | tf_op jit(solution)/shard_map/while/body/eval_jaxpr/ak,aq->kq/dot_general | solution.py:54
  90.6 2.9 %fusion.239 = f32[8,512,8]{1,2,0:T(8,128)} fusion(f32[8,512,8]{1,2,0:T(8,128)} %get-tuple-element.608, s32[]{:T(128)} %get-tuple-element.606, f32[256,8]{0,1:T(8,128)S(1)} %get-tuple-element.625, f32[512]{0:T(512)S(1)} %bitcast.308, f32[256]{0:T(256)S(1)} %bitcast.319, f32[512]{0:T(512)S(1)} %bitcast.306, f32[256]{0:T(256)S(1)} %bitcast.321, ...), kind=kOutput, calls=%fused_computation.74.clone.1 | convolution fusion | flops 13238272 | bytes 34304 | tf_op jit(solution)/shard_map/while/body/eval_jaxpr/ak,aq->kq/dot_general | solution.py:55
  93.5 2.9 %fusion.238 = f32[8,512,8]{1,2,0:T(8,128)} fusion(f32[8,512,8]{1,2,0:T(8,128)} %get-tuple-element.607, s32[]{:T(128)} %get-tuple-element.606, f32[256,8]{0,1:T(8,128)S(1)} %get-tuple-element.625, f32[512]{0:T(512)S(1)} %bitcast.309, f32[256]{0:T(256)S(1)} %bitcast.320, f32[512]{0:T(512)S(1)} %bitcast.307, f32[256]{0:T(256)S(1)} %bitcast.322, ...), kind=kOutput, calls=%fused_computation.76.clone.1 | convolution fusion | flops 13238272 | bytes 34304 | tf_op jit(solution)/shard_map/while/body/eval_jaxpr/ak,aq->kq/dot_general | solution.py:54
  97.7 2.9 %fusion.239 = f32[8,512,8]{1,2,0:T(8,128)} fusion(f32[8,512,8]{1,2,0:T(8,128)} %get-tuple-element.608, s32[]{:T(128)} %get-tuple-element.606, f32[256,8]{0,1:T(8,128)S(1)} %get-tuple-element.625, f32[512]{0:T(512)S(1)} %bitcast.308, f32[256]{0:T(256)S(1)} %bitcast.319, f32[512]{0:T(512)S(1)} %bitcast.306, f32[256]{0:T(256)S(1)} %bitcast.321, ...), kind=kOutput, calls=%fused_computation.74.clone.1 | convolution fusion | flops 13238272 | bytes 34304 | tf_op jit(solution)/shard_map/while/body/eval_jaxpr/ak,aq->kq/dot_general | solution.py:55
  100.6 2.9 %fusion.238 = f32[8,512,8]{1,2,0:T(8,128)} fusion(f32[8,512,8]{1,2,0:T(8,128)} %get-tuple-element.607, s32[]{:T(128)} %get-tuple-element.606, f32[256,8]{0,1:T(8,128)S(1)} %get-tuple-element.625, f32[512]{0:T(512)S(1)} %bitcast.309, f32[256]{0:T(256)S(1)} %bitcast.320, f32[512]{0:T(512)S(1)} %bitcast.307, f32[256]{0:T(256)S(1)} %bitcast.322, ...), kind=kOutput, calls=%fused_computation.76.clone.1 | convolution fusion | flops 13238272 | bytes 34304 | tf_op jit(solution)/shard_map/while/body/eval_jaxpr/ak,aq->kq/dot_general | solution.py:54
  104.3 2.6 collective-permute-start.7
  106.9 48.9 %all-reduce.5.cloned.1.call-done = (f32[4096,8]{0,1:T(8,128)}, f32[4096,8]{0,1:T(8,128)}) async-done(((f32[4096,8]{0,1:T(8,128)}, f32[4096,8]{0,1:T(8,128)}), (f32[4096,8]{0,1:T(8,128)}, f32[4096,8]{0,1:T(8,128)})) %all-reduce.5.cloned.1.call-update) | async-done | bytes 262160 | tf_op jit(solution)/shard_map/psum | solution.py:338
  156.9 57.3 %while.36 = (s32[]{:T(128)}, bf16[4,64,512]{2,1,0:T(8,128)(2,1)S(1)}, f32[4,64,640]{2,1,0:T(8,128)S(1)}, s32[4,64,64]{2,1,0:T(8,128)S(1)}, f32[3,384]{1,0:T(4,12...) while((s32[]{:T(128)}, ...), condition=%wide.region_6.7_spmd, body=%wide.region_0.6_spmd.sunk | while | flops 2032549888 | bytes 45476804 | solution.py:359
  157.4 3.1 %multiply_reduce_fusion.7 = (f32[4096]{0:T(1024)S(1)}, f32[3,4096]{1,0:T(4,128)S(1)}) fusion(f32[3,4096]{1,0:T(4,128)S(1)} %sub.133, f32[3,384]{1,0:T(4,128)S(1)} %get-tuple-element.585, s32[4096]{0:T(1024)S(1)} %eq.279), kind=kOutput, calls=%fused_computation.31.clone.1 | convolution fusion | flops 58228736 | bytes 135680 | tf_op jit(solution)/shard_map/while/body/eval_jaxpr/dot_general | solution.py:111
  161.6 3.3 %multiply_convert_fusion.13 = bf16[4096,512]{1,0:T(8,128)(2,1)} fusion(bf16[64,512]{1,0:T(8,128)(2,1)S(1)} %get-tuple-element.589, f32[4096]{0:T(1024)S(1)} %get-tuple-element.519, bf16[4096,64]{0,1:T(8,128)(2,1)S(1)} %multiply_convert_fusion.12, bf16[2,64,64]{2,1,0:T(8,128)(2,1)S(1)} %get-tuple-element.588), kind=kOutput, calls=%fused_computation.clone.1 | convolution fusion | flops 307494912 | bytes 4816896 | tf_op jit(solution)/shard_map/while/body/eval_jaxpr/dot_general | solution.py:138
  165.4 2.5 fusion.227
  167.9 3.4 %bitcast_reduce_fusion.5 = (f32[64,128]{1,0:T(8,128)S(1)}, f32[64,128]{1,0:T(8,128)S(1)}, f32[64,128]{1,0:T(8,128)S(1)}, f32[64,128]{1,0:T(8,128)S(1)}) fusion(f32[4096,512]{1,0:T(8,128)S(1)} %fusion.227, f32[4096]{0:T(1024)S(1)} %mul.1019, bf16[4096,512]{1,0:T(8,128)(2,1)S(1)} %copy-done.1, f32[4096]{0:T(1024)S(1)} %mul.1020, f32[4096]{0:T(1024)S(1)} %mul.1021), kind=kLoop, calls=%fused_computation.15.clone.1 | loop fusion | flops 13598720 | bytes 12763136 | tf_op jit(solution)/shard_map/while/body/eval_jaxpr/reduce_sum | solution.py:150
  171.7 3.1 %multiply_reduce_fusion.7 = (f32[4096]{0:T(1024)S(1)}, f32[3,4096]{1,0:T(4,128)S(1)}) fusion(f32[3,4096]{1,0:T(4,128)S(1)} %sub.133, f32[3,384]{1,0:T(4,128)S(1)} %get-tuple-element.585, s32[4096]{0:T(1024)S(1)} %eq.279), kind=kOutput, calls=%fused_computation.31.clone.1 | convolution fusion | flops 58228736 | bytes 135680 | tf_op jit(solution)/shard_map/while/body/eval_jaxpr/dot_general | solution.py:111
  175.9 3.3 %multiply_convert_fusion.13 = bf16[4096,512]{1,0:T(8,128)(2,1)} fusion(bf16[64,512]{1,0:T(8,128)(2,1)S(1)} %get-tuple-element.589, f32[4096]{0:T(1024)S(1)} %get-tuple-element.519, bf16[4096,64]{0,1:T(8,128)(2,1)S(1)} %multiply_convert_fusion.12, bf16[2,64,64]{2,1,0:T(8,128)(2,1)S(1)} %get-tuple-element.588), kind=kOutput, calls=%fused_computation.clone.1 | convolution fusion | flops 307494912 | bytes 4816896 | tf_op jit(solution)/shard_map/while/body/eval_jaxpr/dot_general | solution.py:138
  179.7 2.5 fusion.227
  182.2 3.4 %bitcast_reduce_fusion.5 = (f32[64,128]{1,0:T(8,128)S(1)}, f32[64,128]{1,0:T(8,128)S(1)}, f32[64,128]{1,0:T(8,128)S(1)}, f32[64,128]{1,0:T(8,128)S(1)}) fusion(f32[4096,512]{1,0:T(8,128)S(1)} %fusion.227, f32[4096]{0:T(1024)S(1)} %mul.1019, bf16[4096,512]{1,0:T(8,128)(2,1)S(1)} %copy-done.1, f32[4096]{0:T(1024)S(1)} %mul.1020, f32[4096]{0:T(1024)S(1)} %mul.1021), kind=kLoop, calls=%fused_computation.15.clone.1 | loop fusion | flops 13598720 | bytes 12763136 | tf_op jit(solution)/shard_map/while/body/eval_jaxpr/reduce_sum | solution.py:150
  186.0 3.1 %multiply_reduce_fusion.7 = (f32[4096]{0:T(1024)S(1)}, f32[3,4096]{1,0:T(4,128)S(1)}) fusion(f32[3,4096]{1,0:T(4,128)S(1)} %sub.133, f32[3,384]{1,0:T(4,128)S(1)} %get-tuple-element.585, s32[4096]{0:T(1024)S(1)} %eq.279), kind=kOutput, calls=%fused_computation.31.clone.1 | convolution fusion | flops 58228736 | bytes 135680 | tf_op jit(solution)/shard_map/while/body/eval_jaxpr/dot_general | solution.py:111
  190.2 3.3 %multiply_convert_fusion.13 = bf16[4096,512]{1,0:T(8,128)(2,1)} fusion(bf16[64,512]{1,0:T(8,128)(2,1)S(1)} %get-tuple-element.589, f32[4096]{0:T(1024)S(1)} %get-tuple-element.519, bf16[4096,64]{0,1:T(8,128)(2,1)S(1)} %multiply_convert_fusion.12, bf16[2,64,64]{2,1,0:T(8,128)(2,1)S(1)} %get-tuple-element.588), kind=kOutput, calls=%fused_computation.clone.1 | convolution fusion | flops 307494912 | bytes 4816896 | tf_op jit(solution)/shard_map/while/body/eval_jaxpr/dot_general | solution.py:138
  194.0 2.5 fusion.227
  196.5 3.4 %bitcast_reduce_fusion.5 = (f32[64,128]{1,0:T(8,128)S(1)}, f32[64,128]{1,0:T(8,128)S(1)}, f32[64,128]{1,0:T(8,128)S(1)}, f32[64,128]{1,0:T(8,128)S(1)}) fusion(f32[4096,512]{1,0:T(8,128)S(1)} %fusion.227, f32[4096]{0:T(1024)S(1)} %mul.1019, bf16[4096,512]{1,0:T(8,128)(2,1)S(1)} %copy-done.1, f32[4096]{0:T(1024)S(1)} %mul.1020, f32[4096]{0:T(1024)S(1)} %mul.1021), kind=kLoop, calls=%fused_computation.15.clone.1 | loop fusion | flops 13598720 | bytes 12763136 | tf_op jit(solution)/shard_map/while/body/eval_jaxpr/reduce_sum | solution.py:150
  200.3 3.1 %multiply_reduce_fusion.7 = (f32[4096]{0:T(1024)S(1)}, f32[3,4096]{1,0:T(4,128)S(1)}) fusion(f32[3,4096]{1,0:T(4,128)S(1)} %sub.133, f32[3,384]{1,0:T(4,128)S(1)} %get-tuple-element.585, s32[4096]{0:T(1024)S(1)} %eq.279), kind=kOutput, calls=%fused_computation.31.clone.1 | convolution fusion | flops 58228736 | bytes 135680 | tf_op jit(solution)/shard_map/while/body/eval_jaxpr/dot_general | solution.py:111
  204.5 3.3 %multiply_convert_fusion.13 = bf16[4096,512]{1,0:T(8,128)(2,1)} fusion(bf16[64,512]{1,0:T(8,128)(2,1)S(1)} %get-tuple-element.589, f32[4096]{0:T(1024)S(1)} %get-tuple-element.519, bf16[4096,64]{0,1:T(8,128)(2,1)S(1)} %multiply_convert_fusion.12, bf16[2,64,64]{2,1,0:T(8,128)(2,1)S(1)} %get-tuple-element.588), kind=kOutput, calls=%fused_computation.clone.1 | convolution fusion | flops 307494912 | bytes 4816896 | tf_op jit(solution)/shard_map/while/body/eval_jaxpr/dot_general | solution.py:138
  208.3 2.5 fusion.227
  210.8 3.4 %bitcast_reduce_fusion.5 = (f32[64,128]{1,0:T(8,128)S(1)}, f32[64,128]{1,0:T(8,128)S(1)}, f32[64,128]{1,0:T(8,128)S(1)}, f32[64,128]{1,0:T(8,128)S(1)}) fusion(f32[4096,512]{1,0:T(8,128)S(1)} %fusion.227, f32[4096]{0:T(1024)S(1)} %mul.1019, bf16[4096,512]{1,0:T(8,128)(2,1)S(1)} %copy-done.1, f32[4096]{0:T(1024)S(1)} %mul.1020, f32[4096]{0:T(1024)S(1)} %mul.1021), kind=kLoop, calls=%fused_computation.15.clone.1 | loop fusion | flops 13598720 | bytes 12763136 | tf_op jit(solution)/shard_map/while/body/eval_jaxpr/reduce_sum | solution.py:150
  216.9 39.2 %while.38 = (s32[]{:T(128)}, f32[256,32]{0,1:T(8,128)S(1)}, f32[3,256]{1,0:T(4,128)S(1)}, f32[3,4096]{1,0:T(4,128)S(1)}, f32[4096,32]{0,1:T(8,128)S(1)}, /*index...) while((s32[]{:T(128)}, f32[256,32]{0,1:T(8,128)S(1)}, ...), condition=%wide.region_15.16_spmd.clone, body=%wide.region_14.15_spmd.clone.sunk | while | flops 101998600 | bytes 299225 | solution.py:86
  219.4 2.4 convolution_add_fusion.9
  224.3 2.4 convolution_add_fusion.9
  234.1 2.4 convolution_add_fusion.9
  243.9 2.4 convolution_add_fusion.9
  253.7 2.4 convolution_add_fusion.9
  257.8 3.3 %all-to-all-start.2 = ((f32[8,4,128]{2,1,0:T(4,128)}), f32[8,4,128]{2,1,0:T(4,128)S(1)}, u32[]{:S(2)}, u32[]{:S(2)}) async-start(f32[8,4,128]{2,1,0:T(4,128)} %copy.79), calls=%async_computation.2 | async-start | bytes 32768 | tf_op jit(solution)/shard_map/all_to_all | solution.py:386
  261.3 4.5 %all-to-all-done.2 = f32[8,4,128]{2,1,0:T(4,128)S(1)} async-done(((f32[8,4,128]{2,1,0:T(4,128)}), f32[8,4,128]{2,1,0:T(4,128)S(1)}, u32[]{:S(2)}, u32[]{:S(2)}) %all-to-all-start.2) | async-done | bytes 16416 | tf_op jit(solution)/shard_map/all_to_all | solution.py:386
  (303 shorter events, 68.6 us)
Async XLA Ops:
  7.2 11.3 %copy-start = (bf16[256,512]{1,0:T(8,128)(2,1)S(1)}, bf16[256,512]{1,0:T(8,128)(2,1)}, u32[]{:S(2)}) copy-start(bf16[256,512]{1,0:T(8,128)(2,1)} %param.30) | copy-start | bytes 786436
  7.2 13.1 %copy-start.14 = (f32[3]{0:T(128)S(1)}, f32[3]{0:T(128)}, u32[]{:S(2)}) copy-start(f32[3]{0:T(128)} %constant.114.clone) | copy-start | bytes 40
  7.2 13.1 %copy-start.6 = (s32[3,4096]{1,0:T(4,128)S(1)}, s32[3,4096]{1,0:T(4,128)}, u32[]{:S(2)}) copy-start(s32[3,4096]{1,0:T(4,128)} %param.36) | copy-start | bytes 147460
  12.4 10.0 %all-to-all-start = ((bf16[8,8,128]{2,1,0:T(8,128)(2,1)}), bf16[8,8,128]{2,1,0:T(8,128)(2,1)S(1)}, u32[]{:S(2)}, u32[]{:S(2)}) async-start(bf16[8,8,128]{2,1,0:T(8,128)(2,1)} %copy.64), calls=%async_computation | async-start | bytes 32768 | tf_op jit(solution)/shard_map/all_to_all | solution.py:293
  18.5 3.4 %copy-start.2 = (s32[256,64]{0,1:T(8,128)S(1)}, s32[256,64]{0,1:T(8,128)}, u32[]{:S(2)}) copy-start(s32[256,64]{0,1:T(8,128)} %param.34) | copy-start | bytes 196612
  19.8 2.3 copy-start.12
  20.6 6.1 %copy-start.13 = (s32[32]{0:T(128)S(1)}, s32[32]{0:T(128)}, u32[]{:S(2)}) copy-start(s32[32]{0:T(128)} %param.33) | copy-start | bytes 388
  20.6 10.4 %copy-start.7 = (f32[6,640]{1,0:T(8,128)S(1)}, f32[6,640]{1,0:T(8,128)}, u32[]{:S(2)}) copy-start(f32[6,640]{1,0:T(8,128)} %param.41) | copy-start | bytes 46084
  22.3 19.4 %all-to-all-start.1 = ((bf16[8,128,512]{2,1,0:T(8,128)(2,1)}), bf16[8,128,512]{2,1,0:T(8,128)(2,1)S(1)}, u32[]{:S(2)}, u32[]{:S(2)}) async-start(bf16[8,128,512]{2,1,0:T(8,128)(2,1)} %copy.71), calls=%async_computation.1 | async-start | bytes 2097152 | tf_op jit(solution)/shard_map/all_to_all | solution.py:294
  26.4 20.3 %copy-start.17 = (bf16[128,8]{0,1:T(8,128)(2,1)S(1)}, bf16[128,8]{0,1:T(8,128)(2,1)}, u32[]{:S(2)}) copy-start(bf16[128,8]{0,1:T(8,128)(2,1)} %param.44) | copy-start | bytes 6148
  26.4 129.5 %all-reduce.5.cloned.1.call-start = ((), (), s32[]{:S(2)}) async-start(), calls=%async_computation.3 | async-start | bytes 524288 | tf_op jit(solution)/shard_map/psum | solution.py:338
  26.9 5.4 %collective-permute-start = (bf16[1,1,3,32]{3,2,1,0:T(4,128)(2,1)S(1)}, bf16[1,1,3,32]{3,2,1,0:T(4,128)(2,1)S(1)}, u32[]{:S(2)}, u32[]{:S(2)}) collective-permute-start(bf16[1,1,3,32]{3,2,1,0:T(4,128)(2,1)S(1)} %fusion.86), channel_id=1, source_target_pairs={{0,8},{8,16},{16,24},{24,0},{1,9},{9,17},{17,25},{25,1},{2,10},{10... | collective-permute-start | bytes 584 | tf_op jit(solution)/shard_map/ppermute | solution.py:24
  28.5 3.8 %collective-permute-start.1 = (bf16[1,1,3,32]{3,2,1,0:T(4,128)(2,1)S(1)}, bf16[1,1,3,32]{3,2,1,0:T(4,128)(2,1)S(1)}, u32[]{:S(2)}, u32[]{:S(2)}) collective-permute-start(bf16[1,1,3,32]{3,2,1,0:T(4,128)(2,1)S(1)} %fusion.86), channel_id=1, source_target_pairs={{8,0},{16,8},{24,16},{0,24},{9,1},{17,9},{25,17},{1,25},{10,2},{18... | collective-permute-start | bytes 584 | tf_op jit(solution)/shard_map/ppermute | solution.py:25
  32.3 8.9 %collective-permute-start.2 = (bf16[3,1,3,32]{3,2,1,0:T(4,128)(2,1)S(1)}, bf16[3,1,3,32]{3,2,1,0:T(4,128)(2,1)S(1)}, u32[]{:S(2)}, u32[]{:S(2)}) collective-permute-start(bf16[3,1,3,32]{3,2,1,0:T(4,128)(2,1)S(1)} %pad_maximum_fusion.5), channel_id=1, source_target_pairs={{0,1},{1,2},{2,3},{3,4},{4,5},{5,6},{6,7},{7,0},{8,9},{9,10},{10,1... | collective-permute-start | bytes 1736 | tf_op jit(solution)/shard_map/ppermute | solution.py:24
  32.4 8.8 %collective-permute-start.3 = (bf16[3,1,3,32]{3,2,1,0:T(4,128)(2,1)S(1)}, bf16[3,1,3,32]{3,2,1,0:T(4,128)(2,1)S(1)}, u32[]{:S(2)}, u32[]{:S(2)}) collective-permute-start(bf16[3,1,3,32]{3,2,1,0:T(4,128)(2,1)S(1)} %pad_maximum_fusion.5), channel_id=1, source_target_pairs={{1,0},{2,1},{3,2},{4,3},{5,4},{6,5},{7,6},{0,7},{9,8},{10,9},{11,1... | collective-permute-start | bytes 1736 | tf_op jit(solution)/shard_map/ppermute | solution.py:25
  42.8 61.3 %collective-permute-start.4 = (bf16[1,1,32,512]{3,2,1,0:T(8,128)(2,1)S(1)}, bf16[1,1,32,512]{3,2,1,0:T(8,128)(2,1)S(1)}, u32[]{:S(2)}, u32[]{:S(2)}) collective-permute-start(bf16[1,1,32,512]{3,2,1,0:T(8,128)(2,1)S(1)} %fusion.84), channel_id=1, source_target_pairs={{0,8},{8,16},{16,24},{24,0},{1,9},{9,17},{17,25},{25,1},{2,10},{10... | collective-permute-start | bytes 98312 | tf_op jit(solution)/shard_map/ppermute | solution.py:24
  44.4 59.7 %collective-permute-start.5 = (bf16[1,1,32,512]{3,2,1,0:T(8,128)(2,1)S(1)}, bf16[1,1,32,512]{3,2,1,0:T(8,128)(2,1)S(1)}, u32[]{:S(2)}, u32[]{:S(2)}) collective-permute-start(bf16[1,1,32,512]{3,2,1,0:T(8,128)(2,1)S(1)} %fusion.84), channel_id=1, source_target_pairs={{8,0},{16,8},{24,16},{0,24},{9,1},{17,9},{25,17},{1,25},{10,2},{18... | collective-permute-start | bytes 98312 | tf_op jit(solution)/shard_map/ppermute | solution.py:25
  46.8 56.7 %copy-start.3 = (bf16[2,128,128]{2,1,0:T(8,128)(2,1)S(1)}, bf16[2,128,128]{2,1,0:T(8,128)(2,1)}, u32[]{:S(2)}) copy-start(bf16[2,128,128]{2,1,0:T(8,128)(2,1)} %param.43) | copy-start | bytes 196612
  103.7 52.4 %copy-start.4 = (bf16[2,128,128]{2,1,0:T(8,128)(2,1)S(1)}, bf16[2,128,128]{2,1,0:T(8,128)(2,1)}, u32[]{:S(2)}) copy-start(bf16[2,128,128]{2,1,0:T(8,128)(2,1)} %param.40) | copy-start | bytes 196612
  104.1 111.5 %all-reduce.7.cloned.1.call-start = ((), (), s32[]{:S(2)}) async-start(), calls=%async_computation.4 | async-start | bytes 524288 | tf_op jit(solution)/shard_map/psum | solution.py:338
  104.2 52.7 %copy-start.15 = (bf16[64,512]{1,0:T(8,128)(2,1)S(1)}, bf16[64,512]{1,0:T(8,128)(2,1)}, u32[]{:S(2)}) copy-start(bf16[64,512]{1,0:T(8,128)(2,1)} %param.39) | copy-start | bytes 196612
  104.2 52.7 %copy-start.16 = (bf16[2,64,64]{2,1,0:T(8,128)(2,1)S(1)}, bf16[2,64,64]{2,1,0:T(8,128)(2,1)}, u32[]{:S(2)}) copy-start(bf16[2,64,64]{2,1,0:T(8,128)(2,1)} %param.38) | copy-start | bytes 49156
  104.2 52.7 %copy-start.18 = (bf16[8,64]{1,0:T(8,128)(2,1)S(1)}, bf16[8,64]{1,0:T(8,128)(2,1)}, u32[]{:S(2)}) copy-start(bf16[8,64]{1,0:T(8,128)(2,1)} %param.37) | copy-start | bytes 3076
  104.2 51.7 %collective-permute-start.6 = (bf16[3,1,32,512]{3,2,1,0:T(8,128)(2,1)S(1)}, bf16[3,1,32,512]{3,2,1,0:T(8,128)(2,1)S(1)}, u32[]{:S(2)}, u32[]{:S(2)}) collective-permute-start(bf16[3,1,32,512]{3,2,1,0:T(8,128)(2,1)S(1)} %pad_maximum_fusion.3), channel_id=1, source_target_pairs={{0,1},{1,2},{2,3},{3,4},{4,5},{5,6},{6,7},{7,0},{8,9},{9,10},{10,1... | collective-permute-start | bytes 294920 | tf_op jit(solution)/shard_map/ppermute | solution.py:24
  104.3 51.6 %collective-permute-start.7 = (bf16[3,1,32,512]{3,2,1,0:T(8,128)(2,1)S(1)}, bf16[3,1,32,512]{3,2,1,0:T(8,128)(2,1)S(1)}, u32[]{:S(2)}, u32[]{:S(2)}) collective-permute-start(bf16[3,1,32,512]{3,2,1,0:T(8,128)(2,1)S(1)} %pad_maximum_fusion.3), channel_id=1, source_target_pairs={{1,0},{2,1},{3,2},{4,3},{5,4},{6,5},{7,6},{0,7},{9,8},{10,9},{11,1... | collective-permute-start | bytes 294920 | tf_op jit(solution)/shard_map/ppermute | solution.py:25
  156.9 57.5 %copy-start.5 = (bf16[2,128,128]{2,1,0:T(8,128)(2,1)S(1)}, bf16[2,128,128]{2,1,0:T(8,128)(2,1)}, u32[]{:S(2)}) copy-start(bf16[2,128,128]{2,1,0:T(8,128)(2,1)} %param.42) | copy-start | bytes 196612
  165.4 2.5 copy-start.1
  179.7 2.5 copy-start.1
  194.0 2.5 copy-start.1
  208.3 2.5 copy-start.1
  214.3 0.7 copy-start.8
  216.8 39.3 %copy-start.9 = (f32[8,128]{1,0:T(8,128)S(1)}, f32[8,128]{1,0:T(8,128)}, u32[]{:S(2)}) copy-start(f32[8,128]{1,0:T(8,128)} %param.45) | copy-start | bytes 12292
  216.8 39.8 %copy-start.10 = (bf16[128,16]{0,1:T(8,128)(2,1)S(1)}, bf16[128,16]{0,1:T(8,128)(2,1)}, u32[]{:S(2)}) copy-start(bf16[128,16]{0,1:T(8,128)(2,1)} %param.46) | copy-start | bytes 12292
  216.8 39.9 %copy-start.19 = (f32[16]{0:T(128)S(1)}, f32[16]{0:T(128)}, u32[]{:S(2)}) copy-start(f32[16]{0:T(128)} %param.47) | copy-start | bytes 196
  216.8 44.3 %copy-start.20 = (s32[2]{0:T(128)S(1)}, s32[2]{0:T(128)}, u32[]{:S(2)}) copy-start(s32[2]{0:T(128)} %param.32) | copy-start | bytes 28
  216.8 49.0 %copy-start.11 = (s32[2]{0:T(128)S(1)}, s32[2]{0:T(128)}, u32[]{:S(2)}) copy-start(s32[2]{0:T(128)} %param.31) | copy-start | bytes 28
  257.8 8.0 %all-to-all-start.2 = ((f32[8,4,128]{2,1,0:T(4,128)}), f32[8,4,128]{2,1,0:T(4,128)S(1)}, u32[]{:S(2)}, u32[]{:S(2)}) async-start(f32[8,4,128]{2,1,0:T(4,128)} %copy.79), calls=%async_computation.2 | async-start | bytes 32768 | tf_op jit(solution)/shard_map/all_to_all | solution.py:386
Sparse Core Ops, SparseCore 0:
  104.2 51.6 all-reduce.4
  158.2 35.0 all-reduce.6
